TPU v7x, 256 devices: a whole 4x4x8 slice. The times are simulated.
256 devices in a mesh: dp: 4 (over x), expert: 32 (over z, y), tensor: 2 (over core).
Axes of the slice: x: 4, y: 4, z: 8, core: 2. Of those that a mesh axis runs over, the one named last changes fastest.
Arguments:
- queries: bfloat16 [8192, 4096], P(('dp', 'expert'), 'tensor'), may hold values from -8 to 8
- fresh_keys: bfloat16 [8192, 512], P(('dp', 'expert'), 'tensor'), may hold values from -6 to 6
- fresh_values: bfloat16 [8192, 512], P(('dp', 'expert'), 'tensor'), may hold values from -6 to 6
- resident_keys: bfloat16 [128, 2048, 512], P(('dp', 'expert'), None, 'tensor'), may hold values from -8 to 8
- resident_values: bfloat16 [128, 2048, 512], P(('dp', 'expert'), None, 'tensor'), may hold values from -6 to 6
- out_weight: bfloat16 [4096, 2048], P('tensor', 'dp'), may hold values from -0.5 to 0.5
- residual: bfloat16 [8192, 2048], P(('dp', 'expert')), may hold values from -23 to 23
- norm_gain: float32 [2048], replicated, may hold values from 0.1 to 1.9
- expert_ids: int32 [8192, 8], P(('dp', 'expert')), may hold values from 0 to 127, all different within a row; in each aligned block of 64 rows (0 to 63, 64 to 127, ...) at most 6 rows name the same one
- gates: float32 [8192, 8], P(('dp', 'expert')), may hold values from 0.05 to 0.5
- w_gate: bfloat16 [128, 2048, 768], P(('dp', 'expert'), None, 'tensor'), may hold values from -0.125 to 0.125
- w_up: bfloat16 [128, 2048, 768], P(('dp', 'expert'), None, 'tensor'), may hold values from -0.125 to 0.125
- w_down: bfloat16 [128, 768, 2048], P(('dp', 'expert'), 'tensor'), may hold values from -0.21875 to 0.21875
Outputs:
- mixed: bfloat16 [8192, 2048], P(('dp', 'expert'), 'tensor')
Inputs may be any that keep to these rules, and one draw needn't show every extreme that they name: `expert_ids`: within the 64 tokens of one sequence no expert is named by more than 6 tokens, a bound that some block reaches; a token names 8 different experts.
All inputs are finite; a program needn't handle non-finite values.
Results may differ from a plain program's by a relative error of at most 0.0085.
Values may be sent and summed in bfloat16 or wider, within the bound.
No kernel may reach another device: no remote copies, remote signals or barrier semaphores. Data moves between devices by JAX's collectives and lax.ppermute only.
A program may use at most 64 MiB of HBM per device.

v0:
```python
import jax
import jax.numpy as jnp
from jax import lax
from jax.sharding import PartitionSpec as P

D = 2048
HEAD_WIDTH = 128
CAP = 6


def attend_local(queries, fresh_keys, fresh_values, resident_keys, resident_values):
    tokens_here = queries.shape[0]
    kv_here = fresh_keys.shape[1] // HEAD_WIDTH
    query_group = queries.shape[1] // HEAD_WIDTH // kv_here
    context = resident_keys.shape[1]
    query_rows = queries.reshape(tokens_here, kv_here, query_group, HEAD_WIDTH)
    joined_keys = jnp.concatenate([resident_keys[0], fresh_keys], 0).reshape(
        context + tokens_here, kv_here, HEAD_WIDTH
    )
    joined_values = jnp.concatenate([resident_values[0], fresh_values], 0).reshape(
        context + tokens_here, kv_here, HEAD_WIDTH
    )
    score = jnp.einsum(
        "tjgd,sjd->jgts", query_rows, joined_keys, preferred_element_type=jnp.float32
    ) * HEAD_WIDTH ** (-0.5)
    places = jnp.arange(context + tokens_here)
    rows = jnp.arange(tokens_here)
    allowed = (places[None, :] < context) | (places[None, :] - context <= rows[:, None])
    score = jnp.where(allowed, score, jnp.float32(-1e30))
    top_score = jnp.max(score, axis=-1, keepdims=True)
    weight = jnp.exp(score - top_score)
    probs = (weight / jnp.sum(weight, axis=-1, keepdims=True)).astype(jnp.bfloat16)
    attended = jnp.einsum(
        "jgts,sjd->tjgd", probs, joined_values, preferred_element_type=jnp.float32
    )
    return attended.reshape(tokens_here, -1).astype(jnp.bfloat16)


def swap_pair(x):
    return lax.ppermute(x, "tensor", [(0, 1), (1, 0)])


def per_device(
    queries,
    fresh_keys,
    fresh_values,
    resident_keys,
    resident_values,
    out_weight,
    residual,
    norm_gain,
    expert_ids,
    gates,
    w_gate,
    w_up,
    w_down,
):
    tokens_here = residual.shape[0]
    lane = lax.axis_index("tensor")
    half = D // lax.axis_size("tensor")
    groups = lax.axis_size("dp")
    attended = attend_local(queries, fresh_keys, fresh_values, resident_keys, resident_values)
    gathered = lax.all_gather(attended, "dp", axis=0, tiled=True)
    part = jnp.dot(gathered, out_weight, preferred_element_type=jnp.float32)
    part = part.reshape(groups, tokens_here, -1)
    mine = lax.all_to_all(part, "dp", split_axis=0, concat_axis=0, tiled=True)
    mine = mine.transpose(1, 0, 2).reshape(tokens_here, D)
    summed = mine + swap_pair(mine)
    hidden = residual.astype(jnp.float32) + summed
    mean_square = jnp.mean(hidden * hidden, axis=-1, keepdims=True)
    normed = (hidden * lax.rsqrt(mean_square + 1e-06) * norm_gain).astype(jnp.bfloat16)
    hidden_half = lax.dynamic_slice_in_dim(hidden, lane * half, half, 1)
    normed_half = lax.dynamic_slice_in_dim(normed, lane * half, half, 1)
    owners = lax.axis_size("dp") * lax.axis_size("expert")
    onehot = (expert_ids[:, :, None] == jnp.arange(owners)[None, None, :]).astype(jnp.int32)
    per_token = jnp.sum(onehot, axis=1)
    before = jnp.cumsum(per_token, axis=0) - per_token
    slot = jnp.sum(onehot * before[:, None, :], axis=-1)
    code = expert_ids * CAP + slot
    pick = (code[:, :, None] == jnp.arange(owners * CAP)[None, None, :]).astype(jnp.bfloat16)
    spread = jnp.sum(pick, axis=1)
    outgoing = jnp.einsum(
        "tr,tf->rf", spread, normed_half, preferred_element_type=jnp.float32
    ).astype(jnp.bfloat16)
    received = lax.all_to_all(
        outgoing.reshape(owners, CAP, half),
        ("dp", "expert"),
        split_axis=0,
        concat_axis=0,
        tiled=True,
    ).reshape(owners * CAP, half)
    other = swap_pair(received)
    first = jnp.where(lane == 0, received, other)
    second = jnp.where(lane == 0, other, received)
    flat = jnp.concatenate([first, second], axis=1)
    gate_part = jnp.dot(flat, w_gate[0], preferred_element_type=jnp.float32)
    up_part = jnp.dot(flat, w_up[0], preferred_element_type=jnp.float32)
    act = (jax.nn.silu(gate_part) * up_part).astype(jnp.bfloat16)
    result = jnp.dot(act, w_down[0], preferred_element_type=jnp.float32)
    own = lax.dynamic_slice_in_dim(result, lane * half, half, 1)
    theirs = lax.dynamic_slice_in_dim(result, (1 - lane) * half, half, 1)
    expert_out = (own + swap_pair(theirs)).astype(jnp.bfloat16)
    returned = lax.all_to_all(
        expert_out.reshape(owners, CAP, half),
        ("dp", "expert"),
        split_axis=0,
        concat_axis=0,
        tiled=True,
    ).reshape(owners * CAP, half)
    picked = jnp.einsum("tkr,rf->tkf", pick, returned, preferred_element_type=jnp.float32)
    moe = jnp.sum(gates[:, :, None] * picked, axis=1)
    return (hidden_half + moe).astype(jnp.bfloat16)


def solution(mesh):
    return jax.shard_map(
        per_device,
        mesh=mesh,
        in_specs=(
            P(("dp", "expert"), "tensor"),
            P(("dp", "expert"), "tensor"),
            P(("dp", "expert"), "tensor"),
            P(("dp", "expert"), None, "tensor"),
            P(("dp", "expert"), None, "tensor"),
            P("tensor", "dp"),
            P(("dp", "expert"), None),
            P(),
            P(("dp", "expert"), None),
            P(("dp", "expert"), None),
            P(("dp", "expert"), None, "tensor"),
            P(("dp", "expert"), None, "tensor"),
            P(("dp", "expert"), "tensor", None),
        ),
        out_specs=P(("dp", "expert"), "tensor"),
        check_vma=False,
    )
```

profile of v0, /device:TPU:2, one launch (start us, length us, event | category | flops | bytes accessed | tf_op | source)
XLA Modules:
  0.0 256.4 jit_solution(13007185668899665555)
XLA Ops:
  7.1 1.5 copy.47
  8.7 1.3 copy.48
  10.0 0.8 copy.62
  10.8 1.5 copy.44
  12.3 1.3 copy.45
  14.3 0.8 fusion.27
  15.1 4.7 %fusion.48 = f32[2,8,64]{2,1,0:T(8,128)S(1)} fusion(pred[64,2112]{1,0:T(8,128)(4,1)S(1)} %fusion.27, bf16[64,2,128]{2,0,1:T(8,128)(2,1)} %get-tuple-element.9, bf16[2048,2,128]{2,0,1:T(8,128)(2,1)} %copy.48, bf16[64,2,8,128]{3,2,1,0:T(8,128)(2,1)S(1)} %bitcast.82), kind=kOutput, calls=%fused_computation.65 | convolution fusion | flops 564463680 | bytes 1482752 | tf_op jit(solution)/shard_map/sub | solution.py:31
  19.8 5.6 %fusion.14 = bf16[64,2,8,128]{3,0,2,1:T(8,128)(2,1)} fusion(f32[2,8,64]{2,1,0:T(8,128)S(1)} %fusion.48, bf16[64,2,128]{2,0,1:T(8,128)(2,1)} %get-tuple-element.10, bf16[2048,2,128]{2,0,1:T(8,128)(2,1)} %copy.45, pred[64,2112]{1,0:T(8,128)(4,1)S(1)} %fusion.27, bf16[64,2,128]{2,0,1:T(8,128)(2,1)} %get-tuple-element.9, ...), kind=kOutput, calls=%fused_computation.25 | convolution fusion | flops 1122569216 | bytes 2826240 | tf_op jit(solution)/shard_map/jgts,sjd->tjgd/dot_general | solution.py:33
  25.4 1.1 copy.51
  27.4 28.6 %all-gather.2.cloned.1.call-done = bf16[256,2048]{1,0:T(8,128)(2,1)} async-done(((bf16[64,2048]{1,0:T(8,128)(2,1)}), bf16[256,2048]{1,0:T(8,128)(2,1)}) %all-gather.2.cloned.1.call-update) | async-done | bytes 1048592 | tf_op jit(solution)/shard_map/all_gather | solution.py:63
  55.9 2.7 %fusion.51 = f32[256,512]{1,0:T(8,128)} fusion(bf16[256,2048]{1,0:T(8,128)(2,1)} %all-gather.2.cloned.1.call-done, bf16[2048,512]{1,0:T(8,128)(2,1)S(1)} %copy-done), kind=kOutput, calls=%fused_computation.66 | convolution fusion | flops 536870912 | bytes 3670016 | tf_op jit(solution)/shard_map/dot_general | solution.py:64
  58.7 5.3 %all-to-all-start = ((f32[4,64,512]{2,1,0:T(8,128)}), f32[4,64,512]{2,1,0:T(8,128)S(1)}, u32[]{:S(2)}, u32[]{:S(2)}) async-start(f32[4,64,512]{2,1,0:T(8,128)} %bitcast.8), calls=%async_computation | async-start | bytes 1048576 | tf_op jit(solution)/shard_map/all_to_all | solution.py:66
  64.0 6.5 %all-to-all-done = f32[4,64,512]{2,1,0:T(8,128)S(1)} async-done(((f32[4,64,512]{2,1,0:T(8,128)}), f32[4,64,512]{2,1,0:T(8,128)S(1)}, u32[]{:S(2)}, u32[]{:S(2)}) %all-to-all-start) | async-done | bytes 524320 | tf_op jit(solution)/shard_map/all_to_all | solution.py:66
  71.2 1.2 select_reduce_fusion
  73.2 1.2 multiply_reduce_fusion.1
  74.4 1.8 convolution_convert_fusion
  76.2 3.7 %reshape.67 = bf16[128,6,1024]{2,1,0:T(8,128)(2,1)} reshape(bf16[768,1024]{1,0:T(8,128)(2,1)} %convolution_convert_fusion) | data formatting | bytes 3145728 | tf_op jit(solution)/shard_map/reshape | solution.py:86
  79.9 64.9 %all_to_all.15 = bf16[128,6,1024]{2,1,0:T(8,128)(2,1)} all-to-all(bf16[128,6,1024]{2,1,0:T(8,128)(2,1)} %reshape.67), channel_id=1, replica_groups=mesh['dp'=4,'expert'=32,'tensor'=2] {'dp','expert'}, dimensions={0} | all-to-all | bytes 3145728 | tf_op jit(solution)/shard_map/all_to_all | solution.py:85
  144.8 3.7 %reshape.68 = bf16[768,1024]{1,0:T(8,128)(2,1)} reshape(bf16[128,6,1024]{2,1,0:T(8,128)(2,1)} %all_to_all.15) | data formatting | bytes 3145728 | tf_op jit(solution)/shard_map/reshape | solution.py:91
  148.5 3.7 %collective-permute-done.1 = bf16[768,1024]{1,0:T(8,128)(2,1)} collective-permute-done((bf16[768,1024]{1,0:T(8,128)(2,1)}, bf16[768,1024]{1,0:T(8,128)(2,1)}, u32[]{:S(2)}, u32[]{:S(2)}) %collective-permute-start.1) | collective-permute-done | bytes 1572896 | tf_op jit(solution)/shard_map/ppermute | solution.py:40
  152.3 2.1 broadcast_select_fusion.1
  154.4 1.2 copy-done.2
  156.0 2.8 %fusion.6 = f32[768,384]{1,0:T(8,128)} fusion(bf16[768,1024]{1,0:T(8,128)(2,1)S(1)} %get-tuple-element.8, bf16[768,1024]{1,0:T(8,128)(2,1)S(1)} %get-tuple-element.7, bf16[1,2048,384]{2,1,0:T(8,128)(2,1)S(1)} %copy-done.13), kind=kOutput, calls=%fused_computation.12 | convolution fusion | flops 1214251008 | bytes 5898240 | tf_op jit(solution)/shard_map/dot_general | solution.py:97
  158.8 9.3 %fusion.8 = f32[768,2048]{1,0:T(8,128)} fusion(bf16[1,384,2048]{2,1,0:T(8,128)(2,1)} %param.25, f32[768,384]{1,0:T(8,128)} %fusion.6, bf16[768,1024]{1,0:T(8,128)(2,1)} %copy-done.3, bf16[768,1024]{1,0:T(8,128)(2,1)} %copy-done.2, bf16[1,2048,384]{2,1,0:T(8,128)(2,1)} %param.23), kind=kOutput, calls=%fused_computation.15 | convolution fusion | flops 2423980032 | bytes 13762560 | tf_op jit(solution)/shard_map/dot_general | solution.py:99
  168.0 2.3 constant_dynamic-slice_fusion
  170.5 5.5 %collective-permute-done.2 = f32[768,1024]{1,0:T(8,128)S(1)} collective-permute-done((f32[768,1024]{1,0:T(8,128)S(1)}, f32[768,1024]{1,0:T(8,128)S(1)}, u32[]{:S(2)}, u32[]{:S(2)}) %collective-permute-start.2) | collective-permute-done | bytes 3145760 | tf_op jit(solution)/shard_map/ppermute | solution.py:40
  176.1 1.7 add_convert_fusion
  177.7 3.7 %reshape.69 = bf16[128,6,1024]{2,1,0:T(8,128)(2,1)} reshape(bf16[768,1024]{1,0:T(8,128)(2,1)} %add_convert_fusion) | data formatting | bytes 3145728 | tf_op jit(solution)/shard_map/reshape | solution.py:104
  181.4 9.0 %all-to-all-start.2 = ((bf16[128,6,1024]{2,1,0:T(8,128)(2,1)}), bf16[128,6,1024]{2,1,0:T(8,128)(2,1)}, u32[]{:S(2)}, u32[]{:S(2)}) async-start(bf16[128,6,1024]{2,1,0:T(8,128)(2,1)} %reshape.69), calls=%async_computation.2 | async-start | bytes 4194304 | tf_op jit(solution)/shard_map/all_to_all | solution.py:103
  190.6 51.7 %all-to-all-done.2 = bf16[128,6,1024]{2,1,0:T(8,128)(2,1)} async-done(((bf16[128,6,1024]{2,1,0:T(8,128)(2,1)}), bf16[128,6,1024]{2,1,0:T(8,128)(2,1)}, u32[]{:S(2)}, u32[]{:S(2)}) %all-to-all-start.2) | async-done | bytes 1572896 | tf_op jit(solution)/shard_map/all_to_all | solution.py:103
  242.3 3.7 %reshape.73 = bf16[768,1024,1]{1,0,2:T(8,128)(2,1)} reshape(bf16[128,6,1024]{2,1,0:T(8,128)(2,1)} %all-to-all-done.2) | data formatting | bytes 3145728 | tf_op jit(solution)/shard_map/reshape | solution.py:109
  246.0 2.8 %multiply_reduce_fusion = f32[64,1024]{1,0:T(8,128)S(1)} fusion(bf16[768,1024,1]{1,0,2:T(8,128)(2,1)} %reshape.73, f32[64,8]{1,0:T(8,128)S(1)} %copy.53, s32[64,8]{1,0:T(8,128)S(1)} %copy.56), kind=kOutput, calls=%fused_computation.11 | convolution fusion | flops 806682624 | bytes 1839104 | tf_op jit(solution)/shard_map/tkr,rf->tkf/dot_general | solution.py:110
  (50 shorter events, 4.8 us)
Async XLA Ops:
  6.5 49.4 %copy-start = (bf16[2048,512]{1,0:T(8,128)(2,1)S(1)}, bf16[2048,512]{1,0:T(8,128)(2,1)}, u32[]{:S(2)}) copy-start(bf16[2048,512]{1,0:T(8,128)(2,1)} %param.18) | copy-start | bytes 6291460
  6.5 49.4 %all-gather.2.cloned.1.call-start = ((), (), s32[]{:S(2)}) async-start(), calls=%async_computation.3 | async-start | bytes 1310720 | tf_op jit(solution)/shard_map/all_gather | solution.py:63
  7.1 2.9 %copy-start.5 = (bf16[64,2048]{1,0:T(8,128)(2,1)S(1)}, bf16[64,2048]{1,0:T(8,128)(2,1)}, u32[]{:S(2)}) copy-start(bf16[64,2048]{1,0:T(8,128)(2,1)} %param.13) | copy-start | bytes 786436
  10.8 2.9 %copy-start.8 = (bf16[64,256]{1,0:T(8,128)(2,1)S(1)}, bf16[64,256]{1,0:T(8,128)(2,1)}, u32[]{:S(2)}) copy-start(bf16[64,256]{1,0:T(8,128)(2,1)} %param.15) | copy-start | bytes 98308
  10.8 2.9 %copy-start.9 = (bf16[64,256]{1,0:T(8,128)(2,1)S(1)}, bf16[64,256]{1,0:T(8,128)(2,1)}, u32[]{:S(2)}) copy-start(bf16[64,256]{1,0:T(8,128)(2,1)} %param.14) | copy-start | bytes 98308
  10.8 4.3 %copy-start.6 = (bf16[8,8,16,128]{3,2,1,0:T(8,128)(2,1)S(1)}, bf16[8,8,16,128]{3,2,1,0:T(8,128)(2,1)}, u32[]{:S(2)}) copy-start(bf16[8,8,16,128]{3,2,1,0:T(8,128)(2,1)} %copy.62) | copy-start | bytes 786436
  15.1 4.7 %copy-start.4 = (bf16[2048,2,128]{2,0,1:T(8,128)(2,1)S(1)}, bf16[2048,2,128]{2,0,1:T(8,128)(2,1)}, u32[]{:S(2)}) copy-start(bf16[2048,2,128]{2,0,1:T(8,128)(2,1)} %copy.48) | copy-start | bytes 3145732
  27.3 36.6 %copy-start.10 = (s32[64,8]{0,1:T(8,128)S(1)}, s32[64,8]{0,1:T(8,128)}, u32[]{:S(2)}) copy-start(s32[64,8]{0,1:T(8,128)} %param.21) | copy-start | bytes 6148
  58.7 13.9 %copy-start.12 = (f32[2048]{0:T(1024)S(1)}, f32[2048]{0:T(1024)}, u32[]{:S(2)}) copy-start(f32[2048]{0:T(1024)} %param.20) | copy-start | bytes 24580
  58.7 14.5 %copy-start.7 = (bf16[64,2048]{1,0:T(8,128)(2,1)S(1)}, bf16[64,2048]{1,0:T(8,128)(2,1)}, u32[]{:S(2)}) copy-start(bf16[64,2048]{1,0:T(8,128)(2,1)} %param.19) | copy-start | bytes 786436
  58.7 11.9 %all-to-all-start = ((f32[4,64,512]{2,1,0:T(8,128)}), f32[4,64,512]{2,1,0:T(8,128)S(1)}, u32[]{:S(2)}, u32[]{:S(2)}) async-start(f32[4,64,512]{2,1,0:T(8,128)} %bitcast.8), calls=%async_computation | async-start | bytes 1048576 | tf_op jit(solution)/shard_map/all_to_all | solution.py:66
  70.6 2.5 collective-permute-start
  148.5 3.8 %collective-permute-start.1 = (bf16[768,1024]{1,0:T(8,128)(2,1)}, bf16[768,1024]{1,0:T(8,128)(2,1)}, u32[]{:S(2)}, u32[]{:S(2)}) collective-permute-start(bf16[768,1024]{1,0:T(8,128)(2,1)} %reshape.68), channel_id=1, source_target_pairs={{0,1},{1,0},{2,3},{3,2},{4,5},{5,4},{6,7},{7,6},{8,9},{9,8},{10,11... | collective-permute-start | bytes 4718600 | tf_op jit(solution)/shard_map/ppermute | solution.py:40
  148.5 7.5 %copy-start.13 = (bf16[1,2048,384]{2,1,0:T(8,128)(2,1)S(1)}, bf16[1,2048,384]{2,1,0:T(8,128)(2,1)}, u32[]{:S(2)}) copy-start(bf16[1,2048,384]{2,1,0:T(8,128)(2,1)} %param.24) | copy-start | bytes 4718596
  154.3 1.2 copy-start.2
  154.4 1.6 copy-start.3
  168.0 8.0 %copy-start.1 = (f32[768,2048]{1,0:T(8,128)S(1)}, f32[768,2048]{1,0:T(8,128)}, u32[]{:S(2)}) copy-start(f32[768,2048]{1,0:T(8,128)} %fusion.8) | copy-start | bytes 18874372
  170.3 5.7 %collective-permute-start.2 = (f32[768,1024]{1,0:T(8,128)S(1)}, f32[768,1024]{1,0:T(8,128)S(1)}, u32[]{:S(2)}, u32[]{:S(2)}) collective-permute-start(f32[768,1024]{1,0:T(8,128)S(1)} %constant_dynamic-slice_fusion), channel_id=1, source_target_pairs={{0,1},{1,0},{2,3},{3,2},{4,5},{5,4},{6,7},{7,6},{8,9},{9,8},{10,11... | collective-permute-start | bytes 9437192 | tf_op jit(solution)/shard_map/ppermute | solution.py:40
  181.4 9.0 %copy-start.11 = (f32[64,8]{0,1:T(8,128)S(1)}, f32[64,8]{0,1:T(8,128)}, u32[]{:S(2)}) copy-start(f32[64,8]{0,1:T(8,128)} %param.22) | copy-start | bytes 6148
  181.4 60.9 %all-to-all-start.2 = ((bf16[128,6,1024]{2,1,0:T(8,128)(2,1)}), bf16[128,6,1024]{2,1,0:T(8,128)(2,1)}, u32[]{:S(2)}, u32[]{:S(2)}) async-start(bf16[128,6,1024]{2,1,0:T(8,128)(2,1)} %reshape.69), calls=%async_computation.2 | async-start | bytes 4194304 | tf_op jit(solution)/shard_map/all_to_all | solution.py:103
Sparse Core Ops, SparseCore 0:
  27.5 28.4 all-gather.1
where the time goes:
time: 257 us; the launch traced here: 256 us
  waiting for transfers between devices  96.2 us (37%)
  blocking collectives  64.9 us (25%)
  matrix products  29.7 us (12%)
  local copies, waits for them, and re-layouts  28.1 us (11%)
  starting transfers between devices  14.8 us (6%)
  between operations  13.6 us (5%)
  other arithmetic  9.14 us (4%)
    all_to_all x1, blocking collectives, per_device(): lax.all_to_all(outgoing.reshape(owners, CAP, half), ('dp', 'expert'), spl...  64.9 us
    all_to_all x1, waiting for transfers between devices, per_device(): lax.all_to_all(expert_out.reshape(owners, CAP, half), ('dp', 'expert'), s...  51.7 us
    all_gather x1, waiting for transfers between devices, per_device(): gathered = lax.all_gather(attended, 'dp', axis=0, tiled=True)  28.6 us
    dot_general x1, matrix products, per_device(): result = jnp.dot(act, w_down[0], preferred_element_type=jnp.float32)  9.28 us
    ppermute x3, waiting for transfers between devices, swap_pair(): return lax.ppermute(x, 'tensor', [(0, 1), (1, 0)])  9.27 us
    all_to_all x1, starting transfers between devices, per_device(): lax.all_to_all(expert_out.reshape(owners, CAP, half), ('dp', 'expert'), s...  9.03 us
    all_to_all x1, waiting for transfers between devices, per_device(): mine = lax.all_to_all(part, 'dp', split_axis=0, concat_axis=0, tiled=True)  6.54 us
    unnamed x34, local copies, waits for them, and re-layouts  6.45 us
  transfers between devices with their start and end apart: 6, of which 5 were waited for; matrix products, arithmetic and copies ran while one was open for 1% of the time, Pallas kernels for 0%

commit v1 on v0

--- a/solution.py
+++ b/solution.py
@@ -60,7 +60,9 @@
     half = D // lax.axis_size("tensor")
     groups = lax.axis_size("dp")
     attended = attend_local(queries, fresh_keys, fresh_values, resident_keys, resident_values)
-    gathered = lax.all_gather(attended, "dp", axis=0, tiled=True)
+    gathered = jnp.concatenate(
+        lax.all_to_all(jnp.stack([attended] * lax.axis_size("dp")), "dp", 0, 0), axis=0
+    )
     part = jnp.dot(gathered, out_weight, preferred_element_type=jnp.float32)
     part = part.reshape(groups, tokens_here, -1)
     mine = lax.all_to_all(part, "dp", split_axis=0, concat_axis=0, tiled=True)

time: 257 us -> 234 us (0.911)
  waiting for transfers between devices: 96.2 us -> 68.1 us
  blocking collectives: 64.9 us -> 84.8 us
  between operations: 13.6 us -> 0.21 us
    all_gather x1 -> x0, waiting for transfers between devices: 28.6 us -> none  [per_device(): gathered = lax.all_gather(attended, 'dp', axis=0, tiled=True)]
    all_to_all x0 -> x1, blocking collectives: none -> 18.3 us  [per_device(): lax.all_to_all(jnp.stack([attended] * lax.axis_size('dp')), 'dp', 0, 0)]
  transfers between devices with their start and end apart: 6 -> 5, of which waited for: 5 -> 4; matrix products, arithmetic and copies ran while one was open for 1% -> 1% of each run, Pallas kernels for 0% -> 0%
where the time goes in v1:
time: 234 us; the launch traced here: 233 us
  blocking collectives  84.8 us (36%)
  waiting for transfers between devices  68.1 us (29%)
  matrix products  28.4 us (12%)
  local copies, waits for them, and re-layouts  27.5 us (12%)
  starting transfers between devices  14.6 us (6%)
  other arithmetic  9.13 us (4%)
    all_to_all x1, blocking collectives, per_device(): lax.all_to_all(outgoing.reshape(owners, CAP, half), ('dp', 'expert'), spl...  66.6 us
    all_to_all x1, waiting for transfers between devices, per_device(): lax.all_to_all(expert_out.reshape(owners, CAP, half), ('dp', 'expert'), s...  51.7 us
    all_to_all x1, blocking collectives, per_device(): lax.all_to_all(jnp.stack([attended] * lax.axis_size('dp')), 'dp', 0, 0)  18.3 us
    dot_general x1, matrix products, per_device(): result = jnp.dot(act, w_down[0], preferred_element_type=jnp.float32)  9.28 us
    ppermute x3, waiting for transfers between devices, swap_pair(): return lax.ppermute(x, 'tensor', [(0, 1), (1, 0)])  9.27 us
    all_to_all x1, starting transfers between devices, per_device(): lax.all_to_all(expert_out.reshape(owners, CAP, half), ('dp', 'expert'), s...  9.03 us
    all_to_all x1, waiting for transfers between devices, per_device(): mine = lax.all_to_all(part, 'dp', split_axis=0, concat_axis=0, tiled=True)  7.05 us
    unnamed x34, local copies, waits for them, and re-layouts  5.73 us
  transfers between devices with their start and end apart: 5, of which 4 were waited for; matrix products, arithmetic and copies ran while one was open for 1% of the time, Pallas kernels for 0%

profile of v1, /device:TPU:2, one launch (start us, length us, event | category | flops | bytes accessed | tf_op | source)
XLA Modules:
  0.0 232.7 jit_solution(9801580326967590014)
XLA Ops:
  0.6 1.5 copy.46
  2.1 1.3 copy.47
  3.5 0.8 copy.61
  4.3 1.5 copy.43
  5.8 1.3 copy.44
  7.8 0.8 fusion.29
  8.6 4.7 %fusion.50 = f32[2,8,64]{2,1,0:T(8,128)S(1)} fusion(pred[64,2112]{1,0:T(8,128)(4,1)S(1)} %fusion.29, bf16[64,2,128]{2,0,1:T(8,128)(2,1)} %get-tuple-element.9, bf16[2048,2,128]{2,0,1:T(8,128)(2,1)} %copy.47, bf16[64,2,8,128]{3,2,1,0:T(8,128)(2,1)S(1)} %bitcast.83), kind=kOutput, calls=%fused_computation.67 | convolution fusion | flops 564463680 | bytes 1482752 | tf_op jit(solution)/shard_map/sub | solution.py:31
  13.2 5.6 %fusion.16 = bf16[64,2,8,128]{3,0,2,1:T(8,128)(2,1)} fusion(f32[2,8,64]{2,1,0:T(8,128)S(1)} %fusion.50, bf16[64,2,128]{2,0,1:T(8,128)(2,1)} %get-tuple-element.10, bf16[2048,2,128]{2,0,1:T(8,128)(2,1)} %copy.44, pred[64,2112]{1,0:T(8,128)(4,1)S(1)} %fusion.29, bf16[64,2,128]{2,0,1:T(8,128)(2,1)} %get-tuple-element.9, ...), kind=kOutput, calls=%fused_computation.27 | convolution fusion | flops 1122569216 | bytes 2826240 | tf_op jit(solution)/shard_map/jgts,sjd->tjgd/dot_general | solution.py:33
  18.9 1.1 copy.50
  20.2 18.3 %all_to_all.20 = bf16[4,64,2048]{2,1,0:T(8,128)(2,1)S(1)} all-to-all(bf16[4,64,2048]{2,1,0:T(8,128)(2,1)S(1)} %stack.2), channel_id=1, replica_groups=mesh['dp'=4,'expert'=32,'tensor'=2] {'dp'}, dimensions={0} | all-to-all | bytes 2097152 | tf_op jit(solution)/shard_map/all_to_all | solution.py:64
  38.5 1.5 fusion.6
  40.0 5.0 %all-to-all-start.1 = ((f32[4,64,512]{2,1,0:T(8,128)}), f32[4,64,512]{2,1,0:T(8,128)S(1)}, u32[]{:S(2)}, u32[]{:S(2)}) async-start(f32[4,64,512]{2,1,0:T(8,128)} %fusion.6), calls=%async_computation.1 | async-start | bytes 1048576 | tf_op jit(solution)/shard_map/all_to_all | solution.py:68
  45.1 7.0 %all-to-all-done.1 = f32[4,64,512]{2,1,0:T(8,128)S(1)} async-done(((f32[4,64,512]{2,1,0:T(8,128)}), f32[4,64,512]{2,1,0:T(8,128)S(1)}, u32[]{:S(2)}, u32[]{:S(2)}) %all-to-all-start.1) | async-done | bytes 524320 | tf_op jit(solution)/shard_map/all_to_all | solution.py:68
  52.7 1.2 select_reduce_fusion
  54.7 1.2 multiply_reduce_fusion.1
  55.9 1.8 convolution_convert_fusion
  57.7 3.7 %reshape.70 = bf16[128,6,1024]{2,1,0:T(8,128)(2,1)} reshape(bf16[768,1024]{1,0:T(8,128)(2,1)} %convolution_convert_fusion) | data formatting | bytes 3145728 | tf_op jit(solution)/shard_map/reshape | solution.py:88
  61.4 66.6 %all_to_all.21 = bf16[128,6,1024]{2,1,0:T(8,128)(2,1)} all-to-all(bf16[128,6,1024]{2,1,0:T(8,128)(2,1)} %reshape.70), channel_id=1, replica_groups=mesh['dp'=4,'expert'=32,'tensor'=2] {'dp','expert'}, dimensions={0} | all-to-all | bytes 3145728 | tf_op jit(solution)/shard_map/all_to_all | solution.py:87
  128.0 3.7 %reshape.71 = bf16[768,1024]{1,0:T(8,128)(2,1)} reshape(bf16[128,6,1024]{2,1,0:T(8,128)(2,1)} %all_to_all.21) | data formatting | bytes 3145728 | tf_op jit(solution)/shard_map/reshape | solution.py:93
  131.7 3.7 %collective-permute-done.1 = bf16[768,1024]{1,0:T(8,128)(2,1)} collective-permute-done((bf16[768,1024]{1,0:T(8,128)(2,1)}, bf16[768,1024]{1,0:T(8,128)(2,1)}, u32[]{:S(2)}, u32[]{:S(2)}) %collective-permute-start.1) | collective-permute-done | bytes 1572896 | tf_op jit(solution)/shard_map/ppermute | solution.py:40
  135.5 2.1 broadcast_select_fusion.1
  137.6 1.2 copy-done.2
  139.2 2.8 %fusion.8 = f32[768,384]{1,0:T(8,128)} fusion(bf16[768,1024]{1,0:T(8,128)(2,1)S(1)} %get-tuple-element.8, bf16[768,1024]{1,0:T(8,128)(2,1)S(1)} %get-tuple-element.7, bf16[1,2048,384]{2,1,0:T(8,128)(2,1)S(1)} %copy-done.13), kind=kOutput, calls=%fused_computation.14 | convolution fusion | flops 1214251008 | bytes 5898240 | tf_op jit(solution)/shard_map/dot_general | solution.py:99
  142.0 9.3 %fusion.10 = f32[768,2048]{1,0:T(8,128)} fusion(bf16[1,384,2048]{2,1,0:T(8,128)(2,1)} %param.25, f32[768,384]{1,0:T(8,128)} %fusion.8, bf16[768,1024]{1,0:T(8,128)(2,1)} %copy-done.3, bf16[768,1024]{1,0:T(8,128)(2,1)} %copy-done.2, bf16[1,2048,384]{2,1,0:T(8,128)(2,1)} %param.23), kind=kOutput, calls=%fused_computation.17 | convolution fusion | flops 2423980032 | bytes 13762560 | tf_op jit(solution)/shard_map/dot_general | solution.py:101
  151.3 2.3 constant_dynamic-slice_fusion
  153.8 5.5 %collective-permute-done.2 = f32[768,1024]{1,0:T(8,128)S(1)} collective-permute-done((f32[768,1024]{1,0:T(8,128)S(1)}, f32[768,1024]{1,0:T(8,128)S(1)}, u32[]{:S(2)}, u32[]{:S(2)}) %collective-permute-start.2) | collective-permute-done | bytes 3145760 | tf_op jit(solution)/shard_map/ppermute | solution.py:40
  159.3 1.7 add_convert_fusion
  161.0 3.7 %reshape.72 = bf16[128,6,1024]{2,1,0:T(8,128)(2,1)} reshape(bf16[768,1024]{1,0:T(8,128)(2,1)} %add_convert_fusion) | data formatting | bytes 3145728 | tf_op jit(solution)/shard_map/reshape | solution.py:106
  164.7 9.0 %all-to-all-start.3 = ((bf16[128,6,1024]{2,1,0:T(8,128)(2,1)}), bf16[128,6,1024]{2,1,0:T(8,128)(2,1)}, u32[]{:S(2)}, u32[]{:S(2)}) async-start(bf16[128,6,1024]{2,1,0:T(8,128)(2,1)} %reshape.72), calls=%async_computation.3 | async-start | bytes 4194304 | tf_op jit(solution)/shard_map/all_to_all | solution.py:105
  173.8 51.7 %all-to-all-done.3 = bf16[128,6,1024]{2,1,0:T(8,128)(2,1)} async-done(((bf16[128,6,1024]{2,1,0:T(8,128)(2,1)}), bf16[128,6,1024]{2,1,0:T(8,128)(2,1)}, u32[]{:S(2)}, u32[]{:S(2)}) %all-to-all-start.3) | async-done | bytes 1572896 | tf_op jit(solution)/shard_map/all_to_all | solution.py:105
  225.6 3.7 %reshape.77 = bf16[768,1024,1]{1,0,2:T(8,128)(2,1)} reshape(bf16[128,6,1024]{2,1,0:T(8,128)(2,1)} %all-to-all-done.3) | data formatting | bytes 3145728 | tf_op jit(solution)/shard_map/reshape | solution.py:111
  229.3 2.8 %multiply_reduce_fusion = f32[64,1024]{1,0:T(8,128)S(1)} fusion(bf16[768,1024,1]{1,0,2:T(8,128)(2,1)} %reshape.77, f32[64,8]{1,0:T(8,128)S(1)} %copy.52, s32[64,8]{1,0:T(8,128)S(1)} %copy.55), kind=kOutput, calls=%fused_computation.13 | convolution fusion | flops 806682624 | bytes 1839104 | tf_op jit(solution)/shard_map/tkr,rf->tkf/dot_general | solution.py:112
  (49 shorter events, 4.2 us)
Async XLA Ops:
  0.0 38.5 %copy-start = (bf16[2048,512]{1,0:T(8,128)(2,1)S(1)}, bf16[2048,512]{1,0:T(8,128)(2,1)}, u32[]{:S(2)}) copy-start(bf16[2048,512]{1,0:T(8,128)(2,1)} %param.18) | copy-start | bytes 6291460
  0.6 2.9 %copy-start.5 = (bf16[64,2048]{1,0:T(8,128)(2,1)S(1)}, bf16[64,2048]{1,0:T(8,128)(2,1)}, u32[]{:S(2)}) copy-start(bf16[64,2048]{1,0:T(8,128)(2,1)} %param.13) | copy-start | bytes 786436
  4.2 2.9 %copy-start.8 = (bf16[64,256]{1,0:T(8,128)(2,1)S(1)}, bf16[64,256]{1,0:T(8,128)(2,1)}, u32[]{:S(2)}) copy-start(bf16[64,256]{1,0:T(8,128)(2,1)} %param.15) | copy-start | bytes 98308
  4.2 2.9 %copy-start.9 = (bf16[64,256]{1,0:T(8,128)(2,1)S(1)}, bf16[64,256]{1,0:T(8,128)(2,1)}, u32[]{:S(2)}) copy-start(bf16[64,256]{1,0:T(8,128)(2,1)} %param.14) | copy-start | bytes 98308
  4.3 4.3 %copy-start.6 = (bf16[8,8,16,128]{3,2,1,0:T(8,128)(2,1)S(1)}, bf16[8,8,16,128]{3,2,1,0:T(8,128)(2,1)}, u32[]{:S(2)}) copy-start(bf16[8,8,16,128]{3,2,1,0:T(8,128)(2,1)} %copy.61) | copy-start | bytes 786436
  8.6 4.7 %copy-start.4 = (bf16[2048,2,128]{2,0,1:T(8,128)(2,1)S(1)}, bf16[2048,2,128]{2,0,1:T(8,128)(2,1)}, u32[]{:S(2)}) copy-start(bf16[2048,2,128]{2,0,1:T(8,128)(2,1)} %copy.47) | copy-start | bytes 3145732
  38.5 6.5 %copy-start.10 = (s32[64,8]{0,1:T(8,128)S(1)}, s32[64,8]{0,1:T(8,128)}, u32[]{:S(2)}) copy-start(s32[64,8]{0,1:T(8,128)} %param.21) | copy-start | bytes 6148
  40.0 14.2 %copy-start.12 = (f32[2048]{0:T(1024)S(1)}, f32[2048]{0:T(1024)}, u32[]{:S(2)}) copy-start(f32[2048]{0:T(1024)} %param.20) | copy-start | bytes 24580
  40.0 14.7 %copy-start.7 = (bf16[64,2048]{1,0:T(8,128)(2,1)S(1)}, bf16[64,2048]{1,0:T(8,128)(2,1)}, u32[]{:S(2)}) copy-start(bf16[64,2048]{1,0:T(8,128)(2,1)} %param.19) | copy-start | bytes 786436
  40.0 12.2 %all-to-all-start.1 = ((f32[4,64,512]{2,1,0:T(8,128)}), f32[4,64,512]{2,1,0:T(8,128)S(1)}, u32[]{:S(2)}, u32[]{:S(2)}) async-start(f32[4,64,512]{2,1,0:T(8,128)} %fusion.6), calls=%async_computation.1 | async-start | bytes 1048576 | tf_op jit(solution)/shard_map/all_to_all | solution.py:68
  52.2 2.5 %collective-permute-start = (f32[64,2048]{1,0:T(8,128)S(1)}, f32[64,2048]{1,0:T(8,128)}, u32[]{:S(2)}, u32[]{:S(2)}) collective-permute-start(f32[64,2048]{1,0:T(8,128)S(1)} %bitcast.78), channel_id=1, source_target_pairs={{0,1},{1,0},{2,3},{3,2},{4,5},{5,4},{6,7},{7,6},{8,9},{9,8},{10,11... | collective-permute-start | bytes 1572872 | tf_op jit(solution)/shard_map/ppermute | solution.py:40
  131.7 3.8 %collective-permute-start.1 = (bf16[768,1024]{1,0:T(8,128)(2,1)}, bf16[768,1024]{1,0:T(8,128)(2,1)}, u32[]{:S(2)}, u32[]{:S(2)}) collective-permute-start(bf16[768,1024]{1,0:T(8,128)(2,1)} %reshape.71), channel_id=1, source_target_pairs={{0,1},{1,0},{2,3},{3,2},{4,5},{5,4},{6,7},{7,6},{8,9},{9,8},{10,11... | collective-permute-start | bytes 4718600 | tf_op jit(solution)/shard_map/ppermute | solution.py:40
  131.7 7.5 %copy-start.13 = (bf16[1,2048,384]{2,1,0:T(8,128)(2,1)S(1)}, bf16[1,2048,384]{2,1,0:T(8,128)(2,1)}, u32[]{:S(2)}) copy-start(bf16[1,2048,384]{2,1,0:T(8,128)(2,1)} %param.24) | copy-start | bytes 4718596
  137.6 1.2 copy-start.2
  137.6 1.6 copy-start.3
  151.3 8.0 %copy-start.1 = (f32[768,2048]{1,0:T(8,128)S(1)}, f32[768,2048]{1,0:T(8,128)}, u32[]{:S(2)}) copy-start(f32[768,2048]{1,0:T(8,128)} %fusion.10) | copy-start | bytes 18874372
  153.6 5.7 %collective-permute-start.2 = (f32[768,1024]{1,0:T(8,128)S(1)}, f32[768,1024]{1,0:T(8,128)S(1)}, u32[]{:S(2)}, u32[]{:S(2)}) collective-permute-start(f32[768,1024]{1,0:T(8,128)S(1)} %constant_dynamic-slice_fusion), channel_id=1, source_target_pairs={{0,1},{1,0},{2,3},{3,2},{4,5},{5,4},{6,7},{7,6},{8,9},{9,8},{10,11... | collective-permute-start | bytes 9437192 | tf_op jit(solution)/shard_map/ppermute | solution.py:40
  164.7 9.0 %copy-start.11 = (f32[64,8]{0,1:T(8,128)S(1)}, f32[64,8]{0,1:T(8,128)}, u32[]{:S(2)}) copy-start(f32[64,8]{0,1:T(8,128)} %param.22) | copy-start | bytes 6148
  164.7 60.9 %all-to-all-start.3 = ((bf16[128,6,1024]{2,1,0:T(8,128)(2,1)}), bf16[128,6,1024]{2,1,0:T(8,128)(2,1)}, u32[]{:S(2)}, u32[]{:S(2)}) async-start(bf16[128,6,1024]{2,1,0:T(8,128)(2,1)} %reshape.72), calls=%async_computation.3 | async-start | bytes 4194304 | tf_op jit(solution)/shard_map/all_to_all | solution.py:105
